TPU v7x, 32 devices: a whole 2x2x4 slice. The times are simulated.
32 devices in a mesh: parts: 2 (over x), tok: 8 (over z, y), sub: 2 (over core).
Axes of the slice: x: 2, y: 2, z: 4, core: 2. Of those that a mesh axis runs over, the one named last changes fastest.
Arguments:
- video: bfloat16 [16, 48, 16, 768], P('parts', None, ('tok', 'sub')), parts along dimension 0, may hold values from -6 to 6
- norm_gain: float32 [3, 768], replicated, may hold values from 0.1 to 1.9
- qkv_weight: bfloat16 [3, 3, 768, 768], P(None, None, None, 'sub'), may hold values from -0.21875 to 0.21875
- out_weight: bfloat16 [3, 768, 768], P(None, 'sub'), may hold values from -0.21875 to 0.21875
Outputs:
- refined: bfloat16 [16, 48, 16, 768], P('parts', None, ('tok', 'sub')), parts along dimension 0
There are 2 independent parts, one for each index of `parts`. A program takes and returns all parts, laid end to end along the dimension named above; an argument that names none is the same for every part. Nothing has to cross between parts.
All inputs are finite; a program needn't handle non-finite values.
Results may differ from a plain program's by a relative error of at most 0.014.
Values may be sent and summed in bfloat16 or wider, within the bound.
No kernel may reach another device: no remote copies, remote signals or barrier semaphores. Data moves between devices by JAX's collectives and lax.ppermute only.
A program may use at most 64 MiB of HBM per device.

v0:
```python
import math
import jax
import jax.numpy as jnp
from jax import lax
from jax.sharding import PartitionSpec as P

HEAD_DIM = 64
EPSILON = 1e-06


def normalize(tokens, gain):
    values = tokens.astype(jnp.float32)
    scale = lax.rsqrt(jnp.mean(values * values, axis=-1, keepdims=True) + EPSILON)
    return (values * scale * gain).astype(jnp.bfloat16)


def head_norm(values, shape):
    split = values.reshape(shape + (values.shape[-1] // HEAD_DIM, HEAD_DIM))
    scale = lax.rsqrt(jnp.mean(split * split, axis=-1, keepdims=True) + EPSILON)
    return (split * scale).astype(jnp.bfloat16)


def attend(query, key, value, shape):
    query_n = head_norm(query, shape)
    key_n = head_norm(key, shape)
    value_b = value.reshape(query_n.shape).astype(jnp.bfloat16)
    scores = jnp.einsum(
        "plqhe,pmqhe->pqhlm", query_n, key_n, preferred_element_type=jnp.float32
    ) / math.sqrt(HEAD_DIM)
    expo = jnp.exp(scores)
    probs = (expo / jnp.sum(expo, axis=-1, keepdims=True)).astype(jnp.bfloat16)
    mixed = jnp.einsum("pqhlm,pmqhe->plqhe", probs, value_b, preferred_element_type=jnp.float32)
    return mixed.astype(jnp.bfloat16).reshape(query.shape)


def sublayer(tokens, gain, qkv_part, out_part):
    shape = tokens.shape[:3]
    width = tokens.shape[3]
    normed = normalize(tokens, gain)
    flat = normed.reshape(-1, width)
    qkv = jnp.einsum(
        "nd,jde->jne",
        flat,
        lax.all_gather(qkv_part, "sub", axis=2, tiled=True),
        preferred_element_type=jnp.float32,
    )
    mixed = attend(qkv[0], qkv[1], qkv[2], shape)
    update = jnp.dot(
        mixed,
        lax.all_gather(out_part, "sub", axis=0, tiled=True),
        preferred_element_type=jnp.float32,
    ).reshape(tokens.shape)
    return (tokens.astype(jnp.float32) + update).astype(jnp.bfloat16)


def body(video, norm_gain, qkv_weight, out_weight):
    frames, rows, cols, width = video.shape
    state = sublayer(
        video.reshape(1, frames, rows * cols, width), norm_gain[0], qkv_weight[0], out_weight[0]
    ).reshape(video.shape)
    outer = lax.axis_size("tok")
    inner = lax.axis_size("sub")
    devices = outer * inner
    blocks = frames * rows // devices
    stacked = state.reshape(blocks, devices, cols, width)
    items = lax.all_to_all(stacked, ("tok", "sub"), split_axis=1, concat_axis=2, tiled=True)
    lines = items.reshape(items.shape[0], -1, 1, width)
    turned = sublayer(lines, norm_gain[1], qkv_weight[1], out_weight[1]).reshape(items.shape)
    returned = lax.all_to_all(turned, ("tok", "sub"), split_axis=2, concat_axis=1, tiled=True)
    state = returned.reshape(video.shape)
    return sublayer(state, norm_gain[2], qkv_weight[2], out_weight[2])


def solution(mesh):
    in_specs = (
        P("parts", None, ("tok", "sub"), None),
        P(),
        P(None, None, None, "sub"),
        P(None, "sub", None),
    )
    out_specs = P("parts", None, ("tok", "sub"), None)
    return jax.shard_map(body, mesh=mesh, in_specs=in_specs, out_specs=out_specs, check_vma=False)
```

profile of v0, /device:TPU:0, one launch (start us, length us, event | category | flops | bytes accessed | tf_op | source)
XLA Modules:
  0.0 176.2 jit_solution(2934585236718387457)
XLA Ops:
  6.5 5.1 %fusion.56 = (bf16[1,3,768,384]{3,2,1,0:T(8,128)(2,1)}, bf16[1,3,768,384]{3,2,1,0:T(8,128)(2,1)}, bf16[1,3,768,384]{3,2,1,0:T(8,128)(2,1)}) fusion(bf16[3,3,768,384]{3,2,1,0:T(8,128)(2,1)} %param.6), kind=kLoop, calls=%fused_computation.98 | loop fusion | bytes 10616832 | tf_op jit(solution)/shard_map/slice | solution.py:71
  16.3 10.8 %all-gather.13.cloned.1.call-done = bf16[1,3,768,768]{3,2,1,0:T(8,128)(2,1)} async-done(((bf16[1,3,768,384]{3,2,1,0:T(8,128)(2,1)}), bf16[1,3,768,768]{3,2,1,0:T(8,128)(2,1)}) %all-gather.13.cloned.1.call-update) | async-done | bytes 3538960 | tf_op jit(solution)/shard_map/all_gather | solution.py:44
  27.1 3.5 %fusion.9 = f32[3,384,768]{2,1,0:T(8,128)S(1)} fusion(bf16[1,3,768,768]{3,2,1,0:T(8,128)(2,1)} %all-gather.13.cloned.1.call-done, bf16[384,768]{1,0:T(8,128)(2,1)S(1)} %fusion.34), kind=kOutput, calls=%fused_computation.21 | convolution fusion | flops 1358954496 | bytes 7667712 | tf_op jit(solution)/shard_map/nd,jde->jne/dot_general | solution.py:41
  30.7 2.3 %slice_multiply_fusion.5 = (f32[1,384,768]{2,1,0:T(8,128)}, f32[1,384,768]{2,1,0:T(8,128)}, f32[1,384,768]{2,1,0:T(8,128)}, f32[1,384,768]{2,1,0:T(8,128)}) fusion(f32[3,384,768]{2,1,0:T(8,128)S(1)} %fusion.9), kind=kLoop, calls=%fused_computation.97 | loop fusion | flops 589824 | bytes 7077888 | tf_op jit(solution)/shard_map/mul | solution.py:19
  41.8 3.1 %reshape_squeeze.22 = f32[8,48,12,64]{3,2,1,0:T(8,128)} reshape(f32[1,384,768]{2,1,0:T(8,128)} %get-tuple-element.21) | data formatting | bytes 2359296 | tf_op jit(solution)/shard_map/reshape;squeeze | solution.py:18
  44.9 2.8 %convert_element_type.199 = bf16[8,48,12,64]{3,2,1,0:T(8,128)(2,1)} reshape(bf16[1,384,768]{2,1,0:T(8,128)(2,1)} %slice.98) | data formatting | bytes 1179648 | tf_op jit(solution)/shard_map/convert_element_type | solution.py:26
  47.8 4.0 %multiply_convert_fusion.4 = (bf16[8,48,12,64]{3,2,1,0:T(8,128)(2,1)S(1)}, bf16[8,48,12,64]{3,2,1,0:T(8,128)(2,1)S(1)}) fusion(f32[8,48,12,64]{3,2,1,0:T(8,128)} %reshape_squeeze.22, f32[8,48,12]{2,1,0:T(8,128)S(1)} %add_rsqrt_fusion.4, f32[8,48,12,64]{3,2,1,0:T(8,128)S(1)} %reshape_squeeze.21, f32[8,48,12]{2,1,0:T(8,128)S(1)} %copy-done.13), kind=kLoop, calls=%fused_computation.10 | loop fusion | flops 1179648 | bytes 3575808 | tf_op jit(solution)/shard_map/convert_element_type | solution.py:20
  59.2 5.9 %all-to-all-start = ((bf16[24,16,1,768]{3,0,2,1:T(8,128)(2,1)}), bf16[24,16,1,768]{3,0,2,1:T(8,128)(2,1)S(1)}, u32[]{:S(2)}, u32[]{:S(2)}) async-start(bf16[24,16,1,768]{3,0,2,1:T(8,128)(2,1)} %copy.65), calls=%async_computation | async-start | bytes 1179648 | tf_op jit(solution)/shard_map/all_to_all | solution.py:66
  65.7 14.8 %all-to-all-done = bf16[24,16,1,768]{3,0,2,1:T(8,128)(2,1)S(1)} async-done(((bf16[24,16,1,768]{3,0,2,1:T(8,128)(2,1)}), bf16[24,16,1,768]{3,0,2,1:T(8,128)(2,1)S(1)}, u32[]{:S(2)}, u32[]{:S(2)}) %all-to-all-start) | async-done | bytes 589856 | tf_op jit(solution)/shard_map/all_to_all | solution.py:66
  81.3 3.5 %fusion.12 = f32[3,384,768]{2,1,0:T(8,128)S(1)} fusion(bf16[1,3,768,768]{3,2,1,0:T(8,128)(2,1)} %all-gather.17.cloned.1.call-done, bf16[384,768]{1,0:T(8,128)(2,1)S(1)} %fusion.31), kind=kOutput, calls=%fused_computation.22 | convolution fusion | flops 1358954496 | bytes 7667712 | tf_op jit(solution)/shard_map/nd,jde->jne/dot_general | solution.py:41
  85.7 2.4 %slice_multiply_fusion.3 = (f32[1,384,768]{2,1,0:T(8,128)}, f32[1,384,768]{2,1,0:T(8,128)}, f32[1,384,768]{2,1,0:T(8,128)}, f32[1,384,768]{2,1,0:T(8,128)}) fusion(f32[3,384,768]{2,1,0:T(8,128)S(1)} %fusion.12), kind=kLoop, calls=%fused_computation.95 | loop fusion | flops 589824 | bytes 7077888 | tf_op jit(solution)/shard_map/mul | solution.py:19
  92.6 3.1 %mul.295 = f32[24,16,12,64]{3,2,1,0:T(8,128)} reshape(f32[1,384,768]{2,1,0:T(8,128)} %get-tuple-element.16) | data formatting | bytes 2359296 | tf_op jit(solution)/shard_map/mul | solution.py:19
  95.7 2.8 %reduce_sum.114 = f32[24,16,12]{2,1,0:T(8,128)S(1)} reduce(f32[24,16,12,64]{3,2,1,0:T(8,128)} %mul.295, f32[]{:T(128)} %constant.12.clone.1), dimensions={3}, to_apply=%region_6.0 | reduce | flops 290304 | bytes 1198084 | tf_op jit(solution)/shard_map/reduce_sum | solution.py:19
  98.5 3.1 %reshape_squeeze.24 = f32[24,16,12,64]{3,2,1,0:T(8,128)} reshape(f32[1,384,768]{2,1,0:T(8,128)} %get-tuple-element.17) | data formatting | bytes 2359296 | tf_op jit(solution)/shard_map/reshape;squeeze | solution.py:18
  101.6 2.8 %convert_element_type.213 = bf16[24,16,12,64]{3,2,1,0:T(8,128)(2,1)} reshape(bf16[1,384,768]{2,1,0:T(8,128)(2,1)} %slice.97) | data formatting | bytes 1179648 | tf_op jit(solution)/shard_map/convert_element_type | solution.py:26
  114.0 4.5 %all-to-all-start.1 = ((bf16[24,1,16,768]{3,0,1,2:T(8,128)(2,1)}), bf16[24,1,16,768]{3,0,1,2:T(8,128)(2,1)S(1)}, u32[]{:S(2)}, u32[]{:S(2)}) async-start(bf16[24,1,16,768]{3,0,1,2:T(8,128)(2,1)} %copy.72), calls=%async_computation.1 | async-start | bytes 1179648 | tf_op jit(solution)/shard_map/all_to_all | solution.py:69
  119.0 14.8 %all-to-all-done.1 = bf16[24,1,16,768]{3,0,1,2:T(8,128)(2,1)S(1)} async-done(((bf16[24,1,16,768]{3,0,1,2:T(8,128)(2,1)}), bf16[24,1,16,768]{3,0,1,2:T(8,128)(2,1)S(1)}, u32[]{:S(2)}, u32[]{:S(2)}) %all-to-all-start.1) | async-done | bytes 589856 | tf_op jit(solution)/shard_map/all_to_all | solution.py:69
  135.5 3.5 %fusion.15 = f32[3,384,768]{2,1,0:T(8,128)S(1)} fusion(bf16[1,3,768,768]{3,2,1,0:T(8,128)(2,1)} %all-gather.21.cloned.1.call-done, bf16[384,768]{1,0:T(8,128)(2,1)S(1)} %fusion.28), kind=kOutput, calls=%fused_computation.23 | convolution fusion | flops 1358954496 | bytes 7667712 | tf_op jit(solution)/shard_map/nd,jde->jne/dot_general | solution.py:41
  139.0 2.5 %slice_multiply_fusion.1 = (f32[1,384,768]{2,1,0:T(8,128)}, f32[1,384,768]{2,1,0:T(8,128)}, f32[1,384,768]{2,1,0:T(8,128)}, f32[1,384,768]{2,1,0:T(8,128)}) fusion(f32[3,384,768]{2,1,0:T(8,128)S(1)} %fusion.15), kind=kLoop, calls=%fused_computation.93 | loop fusion | flops 589824 | bytes 7077888 | tf_op jit(solution)/shard_map/mul | solution.py:19
  146.8 3.1 %mul.309 = f32[8,48,12,64]{3,2,1,0:T(8,128)} reshape(f32[1,384,768]{2,1,0:T(8,128)} %get-tuple-element.12) | data formatting | bytes 2359296 | tf_op jit(solution)/shard_map/mul | solution.py:19
  149.9 2.8 %reduce_sum.118 = f32[8,48,12]{2,1,0:T(8,128)S(1)} reduce(f32[8,48,12,64]{3,2,1,0:T(8,128)} %mul.309, f32[]{:T(128)} %constant.12.clone.1), dimensions={3}, to_apply=%region_10.0 | reduce | flops 290304 | bytes 1198084 | tf_op jit(solution)/shard_map/reduce_sum | solution.py:19
  154.6 2.1 %slice.96 = bf16[1,384,768]{2,1,0:T(8,128)(2,1)} slice(f32[3,384,768]{2,1,0:T(8,128)} %copy-done.6), slice={[2:3], [0:384], [0:768]} | slice | bytes 1179648 | tf_op jit(solution)/shard_map/slice | solution.py:47
  158.5 2.8 %convert_element_type.227 = bf16[8,48,12,64]{3,2,1,0:T(8,128)(2,1)} reshape(bf16[1,384,768]{2,1,0:T(8,128)(2,1)} %slice.96) | data formatting | bytes 1179648 | tf_op jit(solution)/shard_map/convert_element_type | solution.py:26
  166.6 2.7 %fusion.24 = bf16[8,48,1,768]{3,1,2,0:T(8,128)(2,1)} fusion(f32[8,48,768]{2,1,0:T(8,128)S(1)} %bitcast.97, bf16[8,48,768]{2,1,0:T(8,128)(2,1)S(1)} %dot_general.55, bf16[1,768,768]{2,1,0:T(8,128)(2,1)} %all-gather.23.cloned.1.call-done), kind=kOutput, calls=%fused_computation.36 | convolution fusion | flops 453574656 | bytes 3538944 | tf_op jit(solution)/shard_map/dot_general | solution.py:48
  (104 shorter events, 53.3 us)
Async XLA Ops:
  6.5 20.6 %all-gather.13.cloned.1.call-start = ((), (), s32[]{:S(2)}) async-start(), calls=%async_computation.2 | async-start | bytes 5308416 | tf_op jit(solution)/shard_map/all_gather | solution.py:44
  11.6 1.5 copy-start.9
  11.6 44.5 %all-gather.15.cloned.1.call-start = ((), (), s32[]{:S(2)}) async-start(), calls=%async_computation.3 | async-start | bytes 1769472 | tf_op jit(solution)/shard_map/all_gather | solution.py:50
  14.3 1.4 copy-start.7
  14.3 66.9 %all-gather.17.cloned.1.call-start = ((), (), s32[]{:S(2)}) async-start(), calls=%async_computation.4 | async-start | bytes 5308416 | tf_op jit(solution)/shard_map/all_gather | solution.py:44
  15.1 0.9 copy-start.14
  15.1 95.9 %all-gather.19.cloned.1.call-start = ((), (), s32[]{:S(2)}) async-start(), calls=%async_computation.5 | async-start | bytes 1769472 | tf_op jit(solution)/shard_map/all_gather | solution.py:50
  44.9 2.8 %copy-start.13 = (f32[8,48,12]{2,1,0:T(8,128)S(1)}, f32[8,48,12]{2,1,0:T(8,128)}, u32[]{:S(2)}) copy-start(f32[8,48,12]{2,1,0:T(8,128)} %add_rsqrt_fusion.5) | copy-start | bytes 55300
  51.7 2.0 %copy-start.11 = (bf16[8,48,12,64]{3,2,1,0:T(8,128)(2,1)S(1)}, bf16[8,48,12,64]{3,2,1,0:T(8,128)(2,1)}, u32[]{:S(2)}) copy-start(bf16[8,48,12,64]{3,2,1,0:T(8,128)(2,1)} %convert_element_type.199) | copy-start | bytes 1769476
  55.2 1.1 copy-start.8
  59.2 21.3 %all-to-all-start = ((bf16[24,16,1,768]{3,0,2,1:T(8,128)(2,1)}), bf16[24,16,1,768]{3,0,2,1:T(8,128)(2,1)S(1)}, u32[]{:S(2)}, u32[]{:S(2)}) async-start(bf16[24,16,1,768]{3,0,2,1:T(8,128)(2,1)} %copy.65), calls=%async_computation | async-start | bytes 1179648 | tf_op jit(solution)/shard_map/all_to_all | solution.py:66
  65.1 70.4 %all-gather.21.cloned.1.call-start = ((), (), s32[]{:S(2)}) async-start(), calls=%async_computation.6 | async-start | bytes 5308416 | tf_op jit(solution)/shard_map/all_gather | solution.py:44
  80.4 0.8 copy-start.3
  104.5 1.9 %copy-start = (f32[24,16,12,64]{3,2,1,0:T(8,128)S(1)}, f32[24,16,12,64]{3,2,1,0:T(8,128)}, u32[]{:S(2)}) copy-start(f32[24,16,12,64]{3,2,1,0:T(8,128)} %reshape_squeeze.24) | copy-start | bytes 3538948
  107.4 1.4 copy-start.10
  110.0 1.1 copy-start.4
  114.0 19.9 %all-to-all-start.1 = ((bf16[24,1,16,768]{3,0,1,2:T(8,128)(2,1)}), bf16[24,1,16,768]{3,0,1,2:T(8,128)(2,1)S(1)}, u32[]{:S(2)}, u32[]{:S(2)}) async-start(bf16[24,1,16,768]{3,0,1,2:T(8,128)(2,1)} %copy.72), calls=%async_computation.1 | async-start | bytes 1179648 | tf_op jit(solution)/shard_map/all_to_all | solution.py:69
  118.4 47.8 %all-gather.23.cloned.1.call-start = ((), (), s32[]{:S(2)}) async-start(), calls=%async_computation.7 | async-start | bytes 1769472 | tf_op jit(solution)/shard_map/all_gather | solution.py:50
  134.3 1.0 copy-start.1
  139.0 3.2 %copy-start.6 = (f32[3,384,768]{2,1,0:T(8,128)}, f32[3,384,768]{2,1,0:T(8,128)S(1)}, u32[]{:S(2)}) copy-start(f32[3,384,768]{2,1,0:T(8,128)S(1)} %fusion.15) | copy-start | bytes 10616836
  161.4 1.4 copy-start.5
  162.8 1.4 copy-start.12
  165.3 1.3 copy-start.2
Sparse Core Ops, SparseCore 0:
  11.8 15.3 all-gather.12
  28.6 10.3 all-gather.14
  40.6 13.7 all-gather.16
  55.8 10.3 all-gather.18
  67.7 13.7 all-gather.20
  120.5 10.5 all-gather.22
where the time goes:
time: 177 us; the launch traced here: 176 us
  local copies, waits for them, and re-layouts  57.6 us (33%)
  waiting for transfers between devices  42.4 us (24%)
  other arithmetic  27.5 us (16%)
  matrix products  23.8 us (13%)
  between operations  14 us (8%)
  starting transfers between devices  11 us (6%)
    all_to_all x1, waiting for transfers between devices, body(): lax.all_to_all(turned, ('tok', 'sub'), split_axis=2, concat_axis=1, tiled...  14.8 us
    all_to_all x1, waiting for transfers between devices, body(): lax.all_to_all(stacked, ('tok', 'sub'), split_axis=1, concat_axis=2, tile...  14.8 us
    mul x6, local copies, waits for them, and re-layouts, head_norm(): scale = lax.rsqrt(jnp.mean(split * split, axis=-1, keepdims=True) + EPSILON)  13.5 us
    another operation x6, local copies, waits for them, and re-layouts, head_norm(): split = values.reshape(shape + (values.shape[-1] // HEAD_DIM, HEAD_DIM))  13.4 us
    all_gather x3, waiting for transfers between devices, sublayer(): lax.all_gather(qkv_part, 'sub', axis=2, tiled=True)  10.8 us
    dot_general x3, matrix products, sublayer(): jnp.einsum('nd,jde->jne', flat, lax.all_gather(qkv_part, 'sub', axis=2, t...  10.6 us
    reduce_sum x6, other arithmetic, head_norm(): scale = lax.rsqrt(jnp.mean(split * split, axis=-1, keepdims=True) + EPSILON)  9.11 us
    convert_element_type x5, other arithmetic, head_norm(): return (split * scale).astype(jnp.bfloat16)  8.72 us
  transfers between devices with their start and end apart: 8, of which 3 were waited for; matrix products, arithmetic and copies ran while one was open for 54% of the time, Pallas kernels for 0%

commit v1 on v0

--- a/solution.py
+++ b/solution.py
@@ -6,6 +6,11 @@
 
 HEAD_DIM = 64
 EPSILON = 1e-06
+
+
+def _clear_keys(array_in, ax_name):
+    r_now = jnp.split(array_in, jax.lax.psum(1, ax_name), axis=2)
+    return jnp.concatenate(jax.lax.all_to_all(jnp.stack(r_now), ax_name, 0, 0), axis=1)
 
 
 def normalize(tokens, gain):
@@ -66,7 +71,7 @@
     items = lax.all_to_all(stacked, ("tok", "sub"), split_axis=1, concat_axis=2, tiled=True)
     lines = items.reshape(items.shape[0], -1, 1, width)
     turned = sublayer(lines, norm_gain[1], qkv_weight[1], out_weight[1]).reshape(items.shape)
-    returned = lax.all_to_all(turned, ("tok", "sub"), split_axis=2, concat_axis=1, tiled=True)
+    returned = _clear_keys(turned, ax_name=("tok", "sub"))
     state = returned.reshape(video.shape)
     return sublayer(state, norm_gain[2], qkv_weight[2], out_weight[2])
 

time: 177 us -> 188 us (1.062)
  local copies, waits for them, and re-layouts: 57.6 us -> 67 us
    unnamed x30 -> x45, local copies, waits for them, and re-layouts: 6.08 us -> 14.5 us
  transfers between devices with their start and end apart: 8 -> 8, of which waited for: 3 -> 3; matrix products, arithmetic and copies ran while one was open for 54% -> 57% of each run, Pallas kernels for 0% -> 0%
where the time goes in v1:
time: 188 us; the launch traced here: 187 us
  local copies, waits for them, and re-layouts  67 us (36%)
  waiting for transfers between devices  42.3 us (22%)
  other arithmetic  28.9 us (15%)
  matrix products  23.8 us (13%)
  between operations  14 us (7%)
  starting transfers between devices  10.9 us (6%)
    all_to_all x1, waiting for transfers between devices, _clear_keys(): jax.lax.all_to_all(jnp.stack(r_now), ax_name, 0, 0)  14.8 us
    all_to_all x1, waiting for transfers between devices, body(): lax.all_to_all(stacked, ('tok', 'sub'), split_axis=1, concat_axis=2, tile...  14.8 us
    unnamed x45, local copies, waits for them, and re-layouts  14.5 us
    mul x6, local copies, waits for them, and re-layouts, head_norm(): scale = lax.rsqrt(jnp.mean(split * split, axis=-1, keepdims=True) + EPSILON)  13.4 us
    another operation x6, local copies, waits for them, and re-layouts, head_norm(): split = values.reshape(shape + (values.shape[-1] // HEAD_DIM, HEAD_DIM))  13.4 us
    all_gather x3, waiting for transfers between devices, sublayer(): lax.all_gather(qkv_part, 'sub', axis=2, tiled=True)  10.8 us
    dot_general x3, matrix products, sublayer(): jnp.einsum('nd,jde->jne', flat, lax.all_gather(qkv_part, 'sub', axis=2, t...  10.6 us
    reduce_sum x6, other arithmetic, head_norm(): scale = lax.rsqrt(jnp.mean(split * split, axis=-1, keepdims=True) + EPSILON)  9.78 us
  transfers between devices with their start and end apart: 8, of which 3 were waited for; matrix products, arithmetic and copies ran while one was open for 57% of the time, Pallas kernels for 0%

profile of v1, /device:TPU:0, one launch (start us, length us, event | category | flops | bytes accessed | tf_op | source)
XLA Modules:
  0.0 187.1 jit_solution(112651955643421401)
XLA Ops:
  6.5 5.1 %fusion.57 = (bf16[1,3,768,384]{3,2,1,0:T(8,128)(2,1)}, bf16[1,3,768,384]{3,2,1,0:T(8,128)(2,1)}, bf16[1,3,768,384]{3,2,1,0:T(8,128)(2,1)}) fusion(bf16[3,3,768,384]{3,2,1,0:T(8,128)(2,1)} %param.6), kind=kLoop, calls=%fused_computation.115 | loop fusion | bytes 10616832 | tf_op jit(solution)/shard_map/slice | solution.py:76
  16.3 10.8 %all-gather.13.cloned.1.call-done = bf16[1,3,768,768]{3,2,1,0:T(8,128)(2,1)} async-done(((bf16[1,3,768,384]{3,2,1,0:T(8,128)(2,1)}), bf16[1,3,768,768]{3,2,1,0:T(8,128)(2,1)}) %all-gather.13.cloned.1.call-update) | async-done | bytes 3538960 | tf_op jit(solution)/shard_map/all_gather | solution.py:49
  27.1 3.5 %fusion.9 = f32[3,384,768]{2,1,0:T(8,128)S(1)} fusion(bf16[1,3,768,768]{3,2,1,0:T(8,128)(2,1)} %all-gather.13.cloned.1.call-done, bf16[384,768]{1,0:T(8,128)(2,1)S(1)} %fusion.35), kind=kOutput, calls=%fused_computation.21 | convolution fusion | flops 1358954496 | bytes 7667712 | tf_op jit(solution)/shard_map/nd,jde->jne/dot_general | solution.py:46
  30.7 2.3 %slice_multiply_fusion.5 = (f32[1,384,768]{2,1,0:T(8,128)}, f32[1,384,768]{2,1,0:T(8,128)}, f32[1,384,768]{2,1,0:T(8,128)}, f32[1,384,768]{2,1,0:T(8,128)}) fusion(f32[3,384,768]{2,1,0:T(8,128)S(1)} %fusion.9), kind=kLoop, calls=%fused_computation.114 | loop fusion | flops 589824 | bytes 7077888 | tf_op jit(solution)/shard_map/mul | solution.py:24
  41.9 3.1 %reshape_squeeze.22 = f32[8,48,12,64]{3,2,1,0:T(8,128)} reshape(f32[1,384,768]{2,1,0:T(8,128)} %get-tuple-element.21) | data formatting | bytes 2359296 | tf_op jit(solution)/shard_map/reshape;squeeze | solution.py:23
  44.9 2.8 %convert_element_type.201 = bf16[8,48,12,64]{3,2,1,0:T(8,128)(2,1)} reshape(bf16[1,384,768]{2,1,0:T(8,128)(2,1)} %slice.98) | data formatting | bytes 1179648 | tf_op jit(solution)/shard_map/convert_element_type | solution.py:31
  47.8 4.0 %multiply_convert_fusion.4 = (bf16[8,48,12,64]{3,2,1,0:T(8,128)(2,1)S(1)}, bf16[8,48,12,64]{3,2,1,0:T(8,128)(2,1)S(1)}) fusion(f32[8,48,12,64]{3,2,1,0:T(8,128)} %reshape_squeeze.22, f32[8,48,12]{2,1,0:T(8,128)S(1)} %add_rsqrt_fusion.4, f32[8,48,12,64]{3,2,1,0:T(8,128)S(1)} %reshape_squeeze.21, f32[8,48,12]{2,1,0:T(8,128)S(1)} %copy-done.13), kind=kLoop, calls=%fused_computation.10 | loop fusion | flops 1179648 | bytes 3575808 | tf_op jit(solution)/shard_map/convert_element_type | solution.py:25
  59.2 5.9 %all-to-all-start = ((bf16[24,16,1,768]{3,0,2,1:T(8,128)(2,1)}), bf16[24,16,1,768]{3,0,2,1:T(8,128)(2,1)S(1)}, u32[]{:S(2)}, u32[]{:S(2)}) async-start(bf16[24,16,1,768]{3,0,2,1:T(8,128)(2,1)} %copy.451), calls=%async_computation | async-start | bytes 1179648 | tf_op jit(solution)/shard_map/all_to_all | solution.py:71
  65.7 14.8 %all-to-all-done = bf16[24,16,1,768]{3,0,2,1:T(8,128)(2,1)S(1)} async-done(((bf16[24,16,1,768]{3,0,2,1:T(8,128)(2,1)}), bf16[24,16,1,768]{3,0,2,1:T(8,128)(2,1)S(1)}, u32[]{:S(2)}, u32[]{:S(2)}) %all-to-all-start) | async-done | bytes 589856 | tf_op jit(solution)/shard_map/all_to_all | solution.py:71
  81.3 3.5 %fusion.12 = f32[3,384,768]{2,1,0:T(8,128)S(1)} fusion(bf16[1,3,768,768]{3,2,1,0:T(8,128)(2,1)} %all-gather.17.cloned.1.call-done, bf16[384,768]{1,0:T(8,128)(2,1)S(1)} %fusion.32), kind=kOutput, calls=%fused_computation.22 | convolution fusion | flops 1358954496 | bytes 7667712 | tf_op jit(solution)/shard_map/nd,jde->jne/dot_general | solution.py:46
  84.8 2.4 %slice_multiply_fusion.3 = (f32[1,384,768]{2,1,0:T(8,128)}, f32[1,384,768]{2,1,0:T(8,128)}, f32[1,384,768]{2,1,0:T(8,128)}, f32[1,384,768]{2,1,0:T(8,128)}) fusion(f32[3,384,768]{2,1,0:T(8,128)S(1)} %fusion.12), kind=kLoop, calls=%fused_computation.112 | loop fusion | flops 589824 | bytes 7077888 | tf_op jit(solution)/shard_map/mul | solution.py:24
  92.7 3.1 %mul.293 = f32[24,16,12,64]{3,2,1,0:T(8,128)} reshape(f32[1,384,768]{2,1,0:T(8,128)} %get-tuple-element.16) | data formatting | bytes 2359296 | tf_op jit(solution)/shard_map/mul | solution.py:24
  95.8 3.5 %reduce_sum.114 = f32[24,16,12]{2,1,0:T(8,128)} reduce(f32[24,16,12,64]{3,2,1,0:T(8,128)} %mul.293, f32[]{:T(128)} %constant.12.clone.1), dimensions={3}, to_apply=%region_6.0 | reduce | flops 290304 | bytes 1198084 | tf_op jit(solution)/shard_map/reduce_sum | solution.py:24
  100.2 3.1 %reshape_squeeze.24 = f32[24,16,12,64]{3,2,1,0:T(8,128)} reshape(f32[1,384,768]{2,1,0:T(8,128)} %get-tuple-element.17) | data formatting | bytes 2359296 | tf_op jit(solution)/shard_map/reshape;squeeze | solution.py:23
  103.3 2.8 %convert_element_type.215 = bf16[24,16,12,64]{3,2,1,0:T(8,128)(2,1)} reshape(bf16[1,384,768]{2,1,0:T(8,128)(2,1)} %slice.97) | data formatting | bytes 1179648 | tf_op jit(solution)/shard_map/convert_element_type | solution.py:31
  125.5 4.5 %all-to-all-start.1 = ((bf16[16,24,1,1,768]{4,1,3,2,0:T(8,128)(2,1)}), bf16[16,24,1,1,768]{4,1,3,2,0:T(8,128)(2,1)S(1)}, u32[]{:S(2)}, u32[]{:S(2)}) async-start(bf16[16,24,1,1,768]{4,1,3,2,0:T(8,128)(2,1)} %bitcast_dynamic-update-slice_fusion), calls=%async_computation.1 | async-start | bytes 1179648 | tf_op jit(solution)/shard_map/all_to_all | solution.py:13
  130.5 14.8 %all-to-all-done.1 = bf16[16,24,1,1,768]{4,1,3,2,0:T(8,128)(2,1)S(1)} async-done(((bf16[16,24,1,1,768]{4,1,3,2,0:T(8,128)(2,1)}), bf16[16,24,1,1,768]{4,1,3,2,0:T(8,128)(2,1)S(1)}, u32[]{:S(2)}, u32[]{:S(2)}) %all-to-all-start.1) | async-done | bytes 589856 | tf_op jit(solution)/shard_map/all_to_all | solution.py:13
  146.4 3.5 %fusion.15 = f32[3,384,768]{2,1,0:T(8,128)S(1)} fusion(bf16[1,3,768,768]{3,2,1,0:T(8,128)(2,1)} %all-gather.21.cloned.1.call-done, bf16[384,768]{1,0:T(8,128)(2,1)S(1)} %fusion.29), kind=kOutput, calls=%fused_computation.23 | convolution fusion | flops 1358954496 | bytes 7667712 | tf_op jit(solution)/shard_map/nd,jde->jne/dot_general | solution.py:46
  150.0 2.5 %slice_multiply_fusion.1 = (f32[1,384,768]{2,1,0:T(8,128)}, f32[1,384,768]{2,1,0:T(8,128)}, f32[1,384,768]{2,1,0:T(8,128)}, f32[1,384,768]{2,1,0:T(8,128)}) fusion(f32[3,384,768]{2,1,0:T(8,128)S(1)} %fusion.15), kind=kLoop, calls=%fused_computation.110 | loop fusion | flops 589824 | bytes 7077888 | tf_op jit(solution)/shard_map/mul | solution.py:24
  157.7 3.1 %mul.307 = f32[8,48,12,64]{3,2,1,0:T(8,128)} reshape(f32[1,384,768]{2,1,0:T(8,128)} %get-tuple-element.12) | data formatting | bytes 2359296 | tf_op jit(solution)/shard_map/mul | solution.py:24
  160.8 2.8 %reduce_sum.118 = f32[8,48,12]{2,1,0:T(8,128)S(1)} reduce(f32[8,48,12,64]{3,2,1,0:T(8,128)} %mul.307, f32[]{:T(128)} %constant.12.clone.1), dimensions={3}, to_apply=%region_10.0 | reduce | flops 290304 | bytes 1198084 | tf_op jit(solution)/shard_map/reduce_sum | solution.py:24
  165.5 2.1 %slice.96 = bf16[1,384,768]{2,1,0:T(8,128)(2,1)} slice(f32[3,384,768]{2,1,0:T(8,128)} %copy-done.6), slice={[2:3], [0:384], [0:768]} | slice | bytes 1179648 | tf_op jit(solution)/shard_map/slice | solution.py:52
  169.5 2.8 %convert_element_type.230 = bf16[8,48,12,64]{3,2,1,0:T(8,128)(2,1)} reshape(bf16[1,384,768]{2,1,0:T(8,128)(2,1)} %slice.96) | data formatting | bytes 1179648 | tf_op jit(solution)/shard_map/convert_element_type | solution.py:31
  177.5 2.7 %fusion.24 = bf16[8,48,1,768]{3,1,2,0:T(8,128)(2,1)} fusion(f32[8,48,768]{2,1,0:T(8,128)S(1)} %bitcast.133, bf16[8,48,768]{2,1,0:T(8,128)(2,1)S(1)} %dot_general.55, bf16[1,768,768]{2,1,0:T(8,128)(2,1)} %all-gather.23.cloned.1.call-done), kind=kOutput, calls=%fused_computation.38 | convolution fusion | flops 453574656 | bytes 3538944 | tf_op jit(solution)/shard_map/dot_general | solution.py:53
  (122 shorter events, 63.5 us)
Async XLA Ops:
  6.5 20.6 %all-gather.13.cloned.1.call-start = ((), (), s32[]{:S(2)}) async-start(), calls=%async_computation.2 | async-start | bytes 5308416 | tf_op jit(solution)/shard_map/all_gather | solution.py:49
  11.6 1.5 copy-start.9
  11.6 44.5 %all-gather.15.cloned.1.call-start = ((), (), s32[]{:S(2)}) async-start(), calls=%async_computation.3 | async-start | bytes 1769472 | tf_op jit(solution)/shard_map/all_gather | solution.py:55
  14.4 1.4 copy-start.7
  14.4 66.9 %all-gather.17.cloned.1.call-start = ((), (), s32[]{:S(2)}) async-start(), calls=%async_computation.4 | async-start | bytes 5308416 | tf_op jit(solution)/shard_map/all_gather | solution.py:49
  15.1 0.9 copy-start.14
  15.1 97.4 %all-gather.19.cloned.1.call-start = ((), (), s32[]{:S(2)}) async-start(), calls=%async_computation.5 | async-start | bytes 1769472 | tf_op jit(solution)/shard_map/all_gather | solution.py:55
  44.9 2.8 %copy-start.13 = (f32[8,48,12]{2,1,0:T(8,128)S(1)}, f32[8,48,12]{2,1,0:T(8,128)}, u32[]{:S(2)}) copy-start(f32[8,48,12]{2,1,0:T(8,128)} %add_rsqrt_fusion.5) | copy-start | bytes 55300
  51.7 2.0 %copy-start.10 = (bf16[8,48,12,64]{3,2,1,0:T(8,128)(2,1)S(1)}, bf16[8,48,12,64]{3,2,1,0:T(8,128)(2,1)}, u32[]{:S(2)}) copy-start(bf16[8,48,12,64]{3,2,1,0:T(8,128)(2,1)} %convert_element_type.201) | copy-start | bytes 1769476
  55.2 1.1 copy-start.8
  59.2 21.3 %all-to-all-start = ((bf16[24,16,1,768]{3,0,2,1:T(8,128)(2,1)}), bf16[24,16,1,768]{3,0,2,1:T(8,128)(2,1)S(1)}, u32[]{:S(2)}, u32[]{:S(2)}) async-start(bf16[24,16,1,768]{3,0,2,1:T(8,128)(2,1)} %copy.451), calls=%async_computation | async-start | bytes 1179648 | tf_op jit(solution)/shard_map/all_to_all | solution.py:71
  65.1 81.3 %all-gather.21.cloned.1.call-start = ((), (), s32[]{:S(2)}) async-start(), calls=%async_computation.6 | async-start | bytes 5308416 | tf_op jit(solution)/shard_map/all_gather | solution.py:49
  80.5 0.8 copy-start.3
  106.1 1.9 %copy-start = (f32[24,16,12,64]{3,2,1,0:T(8,128)S(1)}, f32[24,16,12,64]{3,2,1,0:T(8,128)}, u32[]{:S(2)}) copy-start(f32[24,16,12,64]{3,2,1,0:T(8,128)} %reshape_squeeze.24) | copy-start | bytes 3538948
  109.0 1.4 copy-start.11
  111.6 1.1 copy-start.4
  125.5 19.8 %all-to-all-start.1 = ((bf16[16,24,1,1,768]{4,1,3,2,0:T(8,128)(2,1)}), bf16[16,24,1,1,768]{4,1,3,2,0:T(8,128)(2,1)S(1)}, u32[]{:S(2)}, u32[]{:S(2)}) async-start(bf16[16,24,1,1,768]{4,1,3,2,0:T(8,128)(2,1)} %bitcast_dynamic-update-slice_fusion), calls=%async_computation.1 | async-start | bytes 1179648 | tf_op jit(solution)/shard_map/all_to_all | solution.py:13
  130.0 47.2 %all-gather.23.cloned.1.call-start = ((), (), s32[]{:S(2)}) async-start(), calls=%async_computation.7 | async-start | bytes 1769472 | tf_op jit(solution)/shard_map/all_gather | solution.py:55
  145.8 4.1 %copy-start.1 = (f32[24,16,1,1,768]{4,1,0,3,2:T(8,128)}, f32[24,16,1,1,768]{4,1,0,3,2:T(8,128)S(1)}, u32[]{:S(2)}) copy-start(f32[24,16,1,1,768]{4,1,0,3,2:T(8,128)S(1)} %copy.458) | copy-start | bytes 3538948
  149.9 3.2 %copy-start.6 = (f32[3,384,768]{2,1,0:T(8,128)}, f32[3,384,768]{2,1,0:T(8,128)S(1)}, u32[]{:S(2)}) copy-start(f32[3,384,768]{2,1,0:T(8,128)S(1)} %fusion.15) | copy-start | bytes 10616836
  172.3 1.4 copy-start.5
  173.7 1.4 copy-start.12
  176.2 1.3 copy-start.2
Sparse Core Ops, SparseCore 0:
  11.8 15.3 all-gather.12
  28.7 10.3 all-gather.14
  40.6 13.7 all-gather.16
  55.8 10.3 all-gather.18
  67.7 13.7 all-gather.20
  132.0 10.5 all-gather.22
